TPU v7x, 512 devices: a whole 4x4x16 slice. The times are simulated.
512 devices in a mesh: replica: 8 (over y, x_lo), mp: 64 (over z, x_hi, core).
Axes of the slice: x: 4 (x_hi: 2, x_lo: 2; x = x_hi * 2 + x_lo), y: 4, z: 16, core: 2. Of those that a mesh axis runs over, the one named last changes fastest.
Arguments:
- owner_shard: int32 [1024, 256], P(('replica', 'mp')), may hold values from 0 to 63, as said below
- slot_index: int32 [1024, 256], P(('replica', 'mp')), may hold values from 0 to 127
- lengths: int32 [1024], P(('replica', 'mp')), may hold values from 32 to 256
- labels: float32 [1024, 256], P(('replica', 'mp')), may hold values from 0 to 1
- embed_table: bfloat16 [131072, 256], P('mp'), may hold values from -3 to 3
- accumulator: float32 [131072], P('mp'), may hold values from 0.1 to 10
- touched: int32 [8192], P('mp'), may hold values from 0 to 2047, as said below
- w_in: bfloat16 [256, 1024], replicated, may hold values from -0.375 to 0.375
- w_mid: bfloat16 [1024, 1024], replicated, may hold values from -0.1875 to 0.1875
- norm_gain: float32 [1024], replicated, may hold values from 0.5 to 2
- w_out: float32 [1024], replicated, may hold values from -0.1875 to 0.1875
Outputs:
- table_out: bfloat16 [131072, 256], P('mp')
- accum_out: float32 [131072], P('mp')
Inputs may be any that keep to these rules, and one draw needn't show every extreme that they name: `owner_shard`: among the events of one device, every shard is named at most 16 times, and one shard, the same for all devices, is named exactly 16 times by every device. `touched`: the 128 entries of each shard are distinct rows of that shard.
All inputs are finite; a program needn't handle non-finite values.
Results may differ from a plain program's by a relative error of at most 0.0034.
Values may be sent and summed in bfloat16 or wider, within the bound.
A program may use at most 64 MiB of HBM per device.

v0:
```python
import jax
import jax.numpy as jnp
from jax import lax
from jax.sharding import PartitionSpec as P

learn_rate = 1.0


def silu_slope(values):
    sigma_val = jax.nn.sigmoid(values)
    return sigma_val * (1.0 + values * (1.0 - sigma_val))


def encoder_grad(looked_up, labels, live_mask, w_in, w_mid, norm_gain, w_out):
    pre_act = jnp.dot(looked_up, w_in, preferred_element_type=jnp.float32)
    hidden = jax.nn.silu(pre_act)
    inv_rms = lax.rsqrt(jnp.mean(hidden * hidden, axis=-1, keepdims=True) + 1e-06)
    normed = (hidden * inv_rms * norm_gain).astype(jnp.bfloat16)
    mixed = jnp.dot(normed, w_mid, preferred_element_type=jnp.float32)
    output = hidden + jax.nn.silu(mixed)
    logits = jnp.sum(output * w_out, axis=-1)
    d_logit = (jax.nn.sigmoid(logits) - labels) * live_mask
    d_output = d_logit[:, None] * w_out
    d_mixed = (d_output * silu_slope(mixed)).astype(jnp.bfloat16)
    d_normed = jnp.dot(d_mixed, w_mid.T, preferred_element_type=jnp.float32)
    gained = d_normed * norm_gain
    d_hidden = (
        d_output
        + inv_rms * gained
        - hidden * inv_rms**3 * jnp.mean(hidden * gained, axis=-1, keepdims=True)
    )
    d_pre = (d_hidden * silu_slope(pre_act)).astype(jnp.bfloat16)
    return jnp.dot(d_pre, w_in.T, preferred_element_type=jnp.float32).astype(jnp.bfloat16)


def adagrad_rows(grad_rows_in, old_rows, old_acc):
    acc_new = old_acc + jnp.sum(grad_rows_in * grad_rows_in, axis=1)
    new_rows = (
        old_rows.astype(jnp.float32) - learn_rate * grad_rows_in * lax.rsqrt(acc_new)[:, None]
    )
    return (new_rows, acc_new)


def on_device(
    owner_shard,
    slot_index,
    lengths,
    labels,
    embed_table,
    accumulator,
    touched,
    w_in,
    w_mid,
    norm_gain,
    w_out,
):
    mp_count = lax.axis_size("mp")
    samples, length = owner_shard.shape
    events = samples * length
    capacity = max(2, 2 * events // mp_count)
    emb_width = embed_table.shape[1]
    touch_count = touched.shape[0]
    owners = owner_shard.reshape(events)
    slots = slot_index.reshape(events)
    live_mask = (
        (jnp.arange(length, dtype=jnp.int32)[None, :] < lengths[:, None])
        .astype(jnp.float32)
        .reshape(events)
    )
    local_block = embed_table[touched]
    owner_onehot = (owners[:, None] == jnp.arange(mp_count, dtype=jnp.int32)[None, :]).astype(
        jnp.int32
    )
    slot_rank = jnp.sum((jnp.cumsum(owner_onehot, axis=0) - 1) * owner_onehot, axis=1)
    send_pos = owners * capacity + slot_rank
    requests = (
        jnp.full((mp_count * capacity,), -1, jnp.int32)
        .at[send_pos]
        .set(slots)
        .reshape(mp_count, capacity)
    )
    every_block = lax.all_gather(local_block, "mp", axis=0, tiled=True)
    looked_up = every_block[owners * touch_count + slots]
    asked_slots = lax.all_to_all(requests, "mp", split_axis=0, concat_axis=0, tiled=True)
    block_rows = min(events, 512)
    block_count = events // block_rows

    def one_block(pieces):
        return encoder_grad(pieces[0], pieces[1], pieces[2], w_in, w_mid, norm_gain, w_out)

    event_grads = lax.map(
        one_block,
        (
            looked_up.reshape(block_count, block_rows, emb_width),
            labels.reshape(block_count, block_rows),
            live_mask.reshape(block_count, block_rows),
        ),
    ).reshape(events, emb_width)
    outgoing = (
        jnp.zeros((mp_count * capacity, emb_width), jnp.bfloat16)
        .at[send_pos]
        .set(event_grads)
        .reshape(mp_count, capacity, emb_width)
    )
    incoming = lax.all_to_all(outgoing, "mp", split_axis=0, concat_axis=0, tiled=True)
    slot_onehot = (
        asked_slots.reshape(-1)[:, None] == jnp.arange(touch_count, dtype=jnp.int32)[None, :]
    ).astype(jnp.bfloat16)
    grad_block = jnp.einsum(
        "rt,re->te",
        slot_onehot,
        incoming.reshape(-1, emb_width),
        preferred_element_type=jnp.float32,
    )
    touched_acc = accumulator[touched]
    grad_total = lax.psum(grad_block, "replica")
    new_rows, new_acc = adagrad_rows(grad_total, local_block, touched_acc)
    table_out = embed_table.at[touched].set(new_rows.astype(jnp.bfloat16))
    accum_out = accumulator.at[touched].set(new_acc)
    return (table_out, accum_out)


def solution(mesh):
    in_specs = (
        P(("replica", "mp"), None),
        P(("replica", "mp"), None),
        P(("replica", "mp")),
        P(("replica", "mp"), None),
        P("mp", None),
        P("mp"),
        P("mp"),
        P(),
        P(),
        P(),
        P(),
    )
    out_specs = (P("mp", None), P("mp"))
    return jax.shard_map(
        on_device, mesh=mesh, in_specs=in_specs, out_specs=out_specs, check_vma=False
    )
```

profile of v0, /device:TPU:4, one launch (start us, length us, event | category | flops | bytes accessed | tf_op | source)
XLA Modules:
  0.0 320.2 jit_solution(12716276199991593378)
XLA Ops:
  7.2 0.0 copy-start
  7.2 0.0 copy-start.4
  7.2 0.0 copy-start.6
  7.2 0.0 copy-start.12
  7.2 0.0 copy-start.7
  7.2 0.0 copy-start.5
  7.2 0.0 copy-start.11
  7.2 0.0 all-gather.3.cloned.1.call-start
  7.3 1.4 copy.28
  8.6 0.0 copy-done.5
  8.6 0.0 copy-done.11
  8.7 1.5 gather_fusion
  10.1 0.0 all-gather.3.cloned.1.call-update
  10.2 0.0 copy-done.4
  10.2 0.0 copy-done.6
  10.3 1.2 reduce-window.6
  11.5 0.2 slice_reduce_fusion
  11.7 0.1 fusion.19
  11.9 2.4 scatter_custom_fusion
  14.3 0.7 all_to_all.9
  15.0 18.6 %all-to-all-start = ((s32[64,1,16]{2,1,0:T(1,128)}), s32[64,1,16]{2,1,0:T(1,128)S(1)}, u32[]{:S(2)}, u32[]{:S(2)}) async-start(s32[64,1,16]{2,1,0:T(1,128)} %bitcast.3), calls=%async_computation | async-start | bytes 65536 | tf_op jit(solution)/shard_map/all_to_all | solution.py:84
  33.6 0.0 copy-done.12
  33.7 0.1 iota_compare_fusion.4
  33.7 0.0 copy-done.7
  33.8 130.6 %all-gather.3.cloned.1.call-done = bf16[8192,256]{1,0:T(8,128)(2,1)} async-done(((bf16[128,256]{1,0:T(8,128)(2,1)}), bf16[8192,256]{1,0:T(8,128)(2,1)}) %all-gather.3.cloned.1.call-update) | async-done | bytes 4194320 | tf_op jit(solution)/shard_map/all_gather | solution.py:82
  164.3 4.3 %gather_fusion.1 = bf16[512,256]{1,0:T(8,128)(2,1)S(1)} fusion(bf16[8192,256]{1,0:T(8,128)(2,1)} %all-gather.3.cloned.1.call-done, s32[1024]{0:T(1024)S(1)} %pad_clamp_fusion), kind=kCustom, calls=%fused_computation.1 | custom fusion | bytes 526336 | tf_op jit(solution)/shard_map/gather | solution.py:83
  168.6 0.0 copy-start.9
  168.6 0.0 copy-start.10
  168.6 1.9 multiply_reduce_fusion.2
  170.5 0.0 copy-done
  170.5 0.0 copy-done.9
  170.5 0.0 copy-done.10
  170.6 2.3 multiply_reduce_fusion.1
  172.9 0.0 copy-start.8
  172.9 2.0 multiply_reduce_fusion
  174.9 0.0 copy-done.8
  174.9 2.4 convolution_convert_fusion
  177.3 0.0 copy-start.3
  177.3 3.5 %scatter_custom_fusion.1 = bf16[1024,256]{1,0:T(8,128)(2,1)} fusion(s32[512]{0:T(512)S(1)} %bitcast.53, bf16[512,256]{1,0:T(8,128)(2,1)} %convolution_convert_fusion, bf16[]{:T(256)} %constant.35.clone.1), kind=kCustom, calls=%fused_computation.30 | custom fusion | bytes 524800 | tf_op jit(solution)/shard_map/scatter | solution.py:102
  180.9 0.0 all-to-all-done
  180.9 10.8 %all-to-all-start.1 = ((bf16[64,16,256]{2,1,0:T(8,128)(2,1)}), bf16[64,16,256]{2,1,0:T(8,128)(2,1)}, u32[]{:S(2)}, u32[]{:S(2)}) async-start(bf16[64,16,256]{2,1,0:T(8,128)(2,1)} %bitcast.43), calls=%async_computation.1 | async-start | bytes 1048576 | tf_op jit(solution)/shard_map/all_to_all | solution.py:105
  191.7 0.0 all-reduce.2.cloned.1.call-start
  191.7 0.5 broadcast.180
  192.2 0.7 reduce.5
  193.0 0.1 eq.48
  193.1 32.1 %all-to-all-done.1 = bf16[64,16,256]{2,1,0:T(8,128)(2,1)} async-done(((bf16[64,16,256]{2,1,0:T(8,128)(2,1)}), bf16[64,16,256]{2,1,0:T(8,128)(2,1)}, u32[]{:S(2)}, u32[]{:S(2)}) %all-to-all-start.1) | async-done | bytes 524320 | tf_op jit(solution)/shard_map/all_to_all | solution.py:105
  225.2 2.2 fusion.14
  227.3 0.0 all-reduce.2.cloned.1.call-update
  227.4 1.1 gather_fusion.2
  228.5 79.6 %all-reduce.2.cloned.1.call-done = f32[128,256]{1,0:T(8,128)} async-done(((f32[128,256]{1,0:T(8,128)}), f32[128,256]{1,0:T(8,128)}) %all-reduce.2.cloned.1.call-update) | async-done | bytes 131088 | tf_op jit(solution)/shard_map/psum | solution.py:116
  308.2 1.0 multiply_reduce_fusion.3
  309.2 1.0 scatter_fusion
  310.2 0.0 copy-start.1
  310.2 0.0 copy-done.3
  310.2 2.1 scatter_custom_fusion.2
  312.3 0.0 copy-done.1
  312.3 0.0 copy-start.2
  312.4 1.0 copy-done.2
  (21 shorter events, 0.2 us)
Async XLA Ops:
  7.2 163.4 %copy-start = (bf16[1024,1024]{1,0:T(8,128)(2,1)S(1)}, bf16[1024,1024]{1,0:T(8,128)(2,1)}, u32[]{:S(2)}) copy-start(bf16[1024,1024]{1,0:T(8,128)(2,1)} %param.19) | copy-start | bytes 6291460
  7.2 3.0 copy-start.4
  7.2 3.0 copy-start.6
  7.2 26.4 %copy-start.12 = (s32[2]{0:T(128)S(1)}, s32[2]{0:T(128)}, u32[]{:S(2)}) copy-start(s32[2]{0:T(128)} %param.13) | copy-start | bytes 28
  7.2 26.5 %copy-start.7 = (f32[2,256]{1,0:T(2,128)S(1)}, f32[2,256]{1,0:T(2,128)}, u32[]{:S(2)}) copy-start(f32[2,256]{1,0:T(2,128)} %param.14) | copy-start | bytes 6148
  7.2 1.4 copy-start.5
  7.2 1.4 copy-start.11
  7.2 157.1 %all-gather.3.cloned.1.call-start = ((), (), s32[]{:S(2)}) async-start(), calls=%async_computation.3 | async-start | bytes 4259840 | tf_op jit(solution)/shard_map/all_gather | solution.py:82
  15.0 165.8 %all-to-all-start = ((s32[64,1,16]{2,1,0:T(1,128)}), s32[64,1,16]{2,1,0:T(1,128)S(1)}, u32[]{:S(2)}, u32[]{:S(2)}) async-start(s32[64,1,16]{2,1,0:T(1,128)} %bitcast.3), calls=%async_computation | async-start | bytes 65536 | tf_op jit(solution)/shard_map/all_to_all | solution.py:84
  168.6 1.9 copy-start.9
  168.6 1.9 copy-start.10
  172.9 2.0 copy-start.8
  177.3 132.9 %copy-start.3 = (bf16[128,256]{1,0:T(8,128)(2,1)S(1)}, bf16[128,256]{1,0:T(8,128)(2,1)}, u32[]{:S(2)}) copy-start(bf16[128,256]{1,0:T(8,128)(2,1)} %gather_fusion) | copy-start | bytes 196612
  180.9 44.3 %all-to-all-start.1 = ((bf16[64,16,256]{2,1,0:T(8,128)(2,1)}), bf16[64,16,256]{2,1,0:T(8,128)(2,1)}, u32[]{:S(2)}, u32[]{:S(2)}) async-start(bf16[64,16,256]{2,1,0:T(8,128)(2,1)} %bitcast.43), calls=%async_computation.1 | async-start | bytes 1048576 | tf_op jit(solution)/shard_map/all_to_all | solution.py:105
  191.7 116.5 %all-reduce.2.cloned.1.call-start = ((), (), s32[]{:S(2)}) async-start(), calls=%async_computation.2 | async-start | bytes 262144 | tf_op jit(solution)/shard_map/psum | solution.py:116
  310.2 2.1 copy-start.1
  312.3 1.0 copy-start.2
Sparse Core Ops, SparseCore 0:
  11.3 152.9 all-gather.2
  227.5 80.6 all-reduce.1
where the time goes:
time: 321 us; the launch traced here: 320 us
  waiting for transfers between devices  242 us (75%)
  starting transfers between devices  29.5 us (9%)
  local copies, waits for them, and re-layouts  17.8 us (6%)
  between operations  14.4 us (4%)
  matrix products  10.8 us (3%)
  other arithmetic  5.35 us (2%)
    all_gather x1, waiting for transfers between devices, on_device(): every_block = lax.all_gather(local_block, 'mp', axis=0, tiled=True)  131 us
    psum x1, waiting for transfers between devices, on_device(): grad_total = lax.psum(grad_block, 'replica')  79.6 us
    all_to_all x1, waiting for transfers between devices, on_device(): lax.all_to_all(outgoing, 'mp', split_axis=0, concat_axis=0, tiled=True)  32.1 us
    all_to_all x1, starting transfers between devices, on_device(): lax.all_to_all(requests, 'mp', split_axis=0, concat_axis=0, tiled=True)  18.6 us
    all_to_all x1, starting transfers between devices, on_device(): lax.all_to_all(outgoing, 'mp', split_axis=0, concat_axis=0, tiled=True)  10.8 us
  transfers between devices with their start and end apart: 4, of which 3 were waited for; matrix products, arithmetic and copies ran while one was open for 7% of the time, Pallas kernels for 0%

commit v1 on v0

--- a/solution.py
+++ b/solution.py
@@ -113,7 +113,7 @@
         preferred_element_type=jnp.float32,
     )
     touched_acc = accumulator[touched]
-    grad_total = lax.psum(grad_block, "replica")
+    grad_total = jnp.sum(lax.all_gather(grad_block, "replica"), axis=0)
     new_rows, new_acc = adagrad_rows(grad_total, local_block, touched_acc)
     table_out = embed_table.at[touched].set(new_rows.astype(jnp.bfloat16))
     accum_out = accumulator.at[touched].set(new_acc)

time: 321 us -> 279 us (0.87)
  waiting for transfers between devices: 242 us -> 201 us
    psum x1 -> x0, waiting for transfers between devices: 79.6 us -> none  [on_device(): grad_total = lax.psum(grad_block, 'replica')]
    all_gather x0 -> x1, waiting for transfers between devices: none -> 38.7 us  [on_device(): grad_total = jnp.sum(lax.all_gather(grad_block, 'replica'), axis=0)]
  transfers between devices with their start and end apart: 4 -> 4, of which waited for: 3 -> 3; matrix products, arithmetic and copies ran while one was open for 7% -> 8% of each run, Pallas kernels for 0% -> 0%
where the time goes in v1:
time: 279 us
  waiting for transfers between devices  201 us (72%)
  starting transfers between devices  29.5 us (11%)
  local copies, waits for them, and re-layouts  17.5 us (6%)
  between operations  14.4 us (5%)
  matrix products  10.8 us (4%)
  other arithmetic  5.38 us (2%)
    all_gather x1, waiting for transfers between devices, on_device(): every_block = lax.all_gather(local_block, 'mp', axis=0, tiled=True)  131 us
    all_gather x1, waiting for transfers between devices, on_device(): grad_total = jnp.sum(lax.all_gather(grad_block, 'replica'), axis=0)  38.7 us
    all_to_all x1, waiting for transfers between devices, on_device(): lax.all_to_all(outgoing, 'mp', split_axis=0, concat_axis=0, tiled=True)  32.1 us
    all_to_all x1, starting transfers between devices, on_device(): lax.all_to_all(requests, 'mp', split_axis=0, concat_axis=0, tiled=True)  18.6 us
    all_to_all x1, starting transfers between devices, on_device(): lax.all_to_all(outgoing, 'mp', split_axis=0, concat_axis=0, tiled=True)  10.8 us
  transfers between devices with their start and end apart: 4, of which 3 were waited for; matrix products, arithmetic and copies ran while one was open for 8% of the time, Pallas kernels for 0%

profile of v1, /device:TPU:4, one launch (start us, length us, event | category | flops | bytes accessed | tf_op | source)
XLA Modules:
  0.0 278.8 jit_solution(3459734305210951500)
XLA Ops:
  7.2 0.0 copy-start
  7.2 0.0 copy-start.4
  7.2 0.0 copy-start.6
  7.2 0.0 copy-start.12
  7.2 0.0 copy-start.7
  7.2 0.0 copy-start.5
  7.2 0.0 copy-start.11
  7.2 0.0 all-gather.5.cloned.1.call-start
  7.3 1.4 copy.27
  8.6 0.0 copy-done.5
  8.6 0.0 copy-done.11
  8.7 1.5 gather_fusion
  10.1 0.0 all-gather.5.cloned.1.call-update
  10.2 0.0 copy-done.4
  10.2 0.0 copy-done.6
  10.3 1.2 reduce-window.6
  11.5 0.2 slice_reduce_fusion
  11.7 0.1 fusion.19
  11.9 2.4 scatter_custom_fusion
  14.3 0.7 all_to_all.9
  15.0 18.6 %all-to-all-start = ((s32[64,1,16]{2,1,0:T(1,128)}), s32[64,1,16]{2,1,0:T(1,128)S(1)}, u32[]{:S(2)}, u32[]{:S(2)}) async-start(s32[64,1,16]{2,1,0:T(1,128)} %bitcast.3), calls=%async_computation | async-start | bytes 65536 | tf_op jit(solution)/shard_map/all_to_all | solution.py:84
  33.6 0.0 copy-done.12
  33.7 0.1 iota_compare_fusion.4
  33.7 0.0 copy-done.7
  33.8 130.6 %all-gather.5.cloned.1.call-done = bf16[8192,256]{1,0:T(8,128)(2,1)} async-done(((bf16[128,256]{1,0:T(8,128)(2,1)}), bf16[8192,256]{1,0:T(8,128)(2,1)}) %all-gather.5.cloned.1.call-update) | async-done | bytes 4194320 | tf_op jit(solution)/shard_map/all_gather | solution.py:82
  164.3 4.3 %gather_fusion.1 = bf16[512,256]{1,0:T(8,128)(2,1)S(1)} fusion(bf16[8192,256]{1,0:T(8,128)(2,1)} %all-gather.5.cloned.1.call-done, s32[1024]{0:T(1024)S(1)} %pad_clamp_fusion), kind=kCustom, calls=%fused_computation.1 | custom fusion | bytes 526336 | tf_op jit(solution)/shard_map/gather | solution.py:83
  168.6 0.0 copy-start.9
  168.6 0.0 copy-start.10
  168.6 1.9 multiply_reduce_fusion.2
  170.5 0.0 copy-done
  170.5 0.0 copy-done.9
  170.5 0.0 copy-done.10
  170.6 2.3 multiply_reduce_fusion.1
  172.9 0.0 copy-start.8
  172.9 2.0 multiply_reduce_fusion
  174.9 0.0 copy-done.8
  174.9 2.4 convolution_convert_fusion
  177.3 0.0 copy-start.3
  177.3 3.5 %scatter_custom_fusion.1 = bf16[1024,256]{1,0:T(8,128)(2,1)} fusion(s32[512]{0:T(512)S(1)} %bitcast.55, bf16[512,256]{1,0:T(8,128)(2,1)} %convolution_convert_fusion, bf16[]{:T(256)} %constant.35.clone.1), kind=kCustom, calls=%fused_computation.30 | custom fusion | bytes 524800 | tf_op jit(solution)/shard_map/scatter | solution.py:102
  180.9 0.0 all-to-all-done
  180.9 10.8 %all-to-all-start.1 = ((bf16[64,16,256]{2,1,0:T(8,128)(2,1)}), bf16[64,16,256]{2,1,0:T(8,128)(2,1)}, u32[]{:S(2)}, u32[]{:S(2)}) async-start(bf16[64,16,256]{2,1,0:T(8,128)(2,1)} %bitcast.44), calls=%async_computation.1 | async-start | bytes 1048576 | tf_op jit(solution)/shard_map/all_to_all | solution.py:105
  191.7 0.0 all-gather.7.cloned.1.call-start
  191.7 0.5 broadcast.180
  192.2 0.7 reduce.5
  193.0 0.1 eq.48
  193.1 32.1 %all-to-all-done.1 = bf16[64,16,256]{2,1,0:T(8,128)(2,1)} async-done(((bf16[64,16,256]{2,1,0:T(8,128)(2,1)}), bf16[64,16,256]{2,1,0:T(8,128)(2,1)}, u32[]{:S(2)}, u32[]{:S(2)}) %all-to-all-start.1) | async-done | bytes 524320 | tf_op jit(solution)/shard_map/all_to_all | solution.py:105
  225.2 2.2 fusion.14
  227.3 0.0 all-gather.7.cloned.1.call-update
  227.4 1.1 gather_fusion.2
  228.5 38.7 %all-gather.7.cloned.1.call-done = f32[1024,256]{1,0:T(8,128)} async-done(((f32[128,256]{1,0:T(8,128)}), f32[1024,256]{1,0:T(8,128)}) %all-gather.7.cloned.1.call-update) | async-done | bytes 1048592 | tf_op jit(solution)/shard_map/all_gather | solution.py:116
  267.2 1.3 reduce_sum.64
  268.5 0.1 multiply_reduce_fusion.3
  268.6 0.0 copy-done.3
  268.6 1.7 scatter_custom_fusion.2
  270.4 0.0 copy-start.2
  270.4 1.0 scatter_fusion
  271.4 0.0 copy-done.2
  271.4 0.0 copy-start.1
  271.4 0.6 copy-done.1
  (21 shorter events, 0.2 us)
Async XLA Ops:
  7.2 163.4 %copy-start = (bf16[1024,1024]{1,0:T(8,128)(2,1)S(1)}, bf16[1024,1024]{1,0:T(8,128)(2,1)}, u32[]{:S(2)}) copy-start(bf16[1024,1024]{1,0:T(8,128)(2,1)} %param.19) | copy-start | bytes 6291460
  7.2 3.0 %copy-start.4 = (s32[2,256]{1,0:T(2,128)S(1)}, s32[2,256]{1,0:T(2,128)}, u32[]{:S(2)}) copy-start(s32[2,256]{1,0:T(2,128)} %param.11) | copy-start | bytes 6148
  7.2 3.0 %copy-start.6 = (s32[2,256]{1,0:T(2,128)S(1)}, s32[2,256]{1,0:T(2,128)}, u32[]{:S(2)}) copy-start(s32[2,256]{1,0:T(2,128)} %param.12) | copy-start | bytes 6148
  7.2 26.4 %copy-start.12 = (s32[2]{0:T(128)S(1)}, s32[2]{0:T(128)}, u32[]{:S(2)}) copy-start(s32[2]{0:T(128)} %param.13) | copy-start | bytes 28
  7.2 26.5 %copy-start.7 = (f32[2,256]{1,0:T(2,128)S(1)}, f32[2,256]{1,0:T(2,128)}, u32[]{:S(2)}) copy-start(f32[2,256]{1,0:T(2,128)} %param.14) | copy-start | bytes 6148
  7.2 1.4 copy-start.5
  7.2 1.4 copy-start.11
  7.2 157.1 %all-gather.5.cloned.1.call-start = ((), (), s32[]{:S(2)}) async-start(), calls=%async_computation.2 | async-start | bytes 4259840 | tf_op jit(solution)/shard_map/all_gather | solution.py:82
  15.0 165.8 %all-to-all-start = ((s32[64,1,16]{2,1,0:T(1,128)}), s32[64,1,16]{2,1,0:T(1,128)S(1)}, u32[]{:S(2)}, u32[]{:S(2)}) async-start(s32[64,1,16]{2,1,0:T(1,128)} %bitcast.3), calls=%async_computation | async-start | bytes 65536 | tf_op jit(solution)/shard_map/all_to_all | solution.py:84
  168.6 1.9 copy-start.9
  168.6 1.9 copy-start.10
  172.9 2.0 copy-start.8
  177.3 91.3 %copy-start.3 = (bf16[128,256]{1,0:T(8,128)(2,1)S(1)}, bf16[128,256]{1,0:T(8,128)(2,1)}, u32[]{:S(2)}) copy-start(bf16[128,256]{1,0:T(8,128)(2,1)} %gather_fusion) | copy-start | bytes 196612
  180.9 44.3 %all-to-all-start.1 = ((bf16[64,16,256]{2,1,0:T(8,128)(2,1)}), bf16[64,16,256]{2,1,0:T(8,128)(2,1)}, u32[]{:S(2)}, u32[]{:S(2)}) async-start(bf16[64,16,256]{2,1,0:T(8,128)(2,1)} %bitcast.44), calls=%async_computation.1 | async-start | bytes 1048576 | tf_op jit(solution)/shard_map/all_to_all | solution.py:105
  191.7 75.5 %all-gather.7.cloned.1.call-start = ((), (), s32[]{:S(2)}) async-start(), calls=%async_computation.3 | async-start | bytes 1179648 | tf_op jit(solution)/shard_map/all_gather | solution.py:116
  270.4 1.0 copy-start.2
  271.4 0.6 copy-start.1
Sparse Core Ops, SparseCore 0:
  11.3 152.9 all-gather.4
  227.5 39.6 all-gather.6
